TPU v7x, 128 devices: a whole 4x4x4 slice. The times are simulated.
128 devices in a mesh: grp: 4 (over z_hi, core), mem: 32 (over x, y, z_lo).
Axes of the slice: x: 4, y: 4, z: 4 (z_hi: 2, z_lo: 2; z = z_hi * 2 + z_lo), core: 2. Of those that a mesh axis runs over, the one named last changes fastest.
Arguments:
- amplitudes: bfloat16 [384, 1048576], P('mem', 'grp'), may hold values from -6 to 6
- integrals: bfloat16 [1048576, 1024], P(('grp', 'mem')), may hold values from -0.0625 to 0.0625
- irrep_ef: int32 [1048576], P(('grp', 'mem')), may hold values from 0 to 7
- irrep_ab: int32 [1024], replicated, may hold values from 0 to 7
Outputs:
- residual: float32 [384, 1024], P('mem', 'grp')
All inputs are finite; a program needn't handle non-finite values.
Results may differ from a plain program's by a relative error of at most 0.0003.
Values may be sent and summed in bfloat16 or wider, within the bound.
A program may use at most 128 MiB of HBM per device.

v0:
```python
import jax
import jax.numpy as jnp
from jax import lax
from jax.sharding import PartitionSpec as P


def local(amplitudes, integrals, irrep_ef, irrep_ab):
    member_count = lax.axis_size("mem")
    own_rows = amplitudes.shape[0]
    pair_cols = integrals.shape[0]
    allowed = irrep_ef[:, None] == irrep_ab[None, :]
    blocked = jnp.where(allowed, integrals, jnp.zeros_like(integrals))
    shaped = amplitudes.reshape(own_rows, member_count, pair_cols)
    arrived = lax.all_to_all(shaped, "mem", split_axis=1, concat_axis=0, tiled=True)
    partial_value = jnp.dot(
        arrived.reshape(-1, pair_cols), blocked, preferred_element_type=jnp.float32
    )
    row_share = lax.psum_scatter(partial_value, "mem", scatter_dimension=0, tiled=True)
    result = lax.psum_scatter(row_share, "grp", scatter_dimension=1, tiled=True)
    return result


def solution(mesh):
    placed = (P("mem", "grp"), P(("grp", "mem"), None), P(("grp", "mem")), P())
    return jax.shard_map(
        local, mesh=mesh, in_specs=placed, out_specs=P("mem", "grp"), check_vma=False
    )
```

profile of v0, /device:TPU:2, one launch (start us, length us, event | category | flops | bytes accessed | tf_op | source)
XLA Modules:
  0.0 512.8 jit_solution(3858928027774163082)
XLA Ops:
  6.5 0.0 all-reduce.3.cloned.1.call-start
  6.5 11.2 %copy.12 = bf16[2,8,32,8192]{3,2,1,0:T(8,128)(2,1)} copy(bf16[2,8,32,8192]{3,1,2,0:T(8,128)(2,1)} %bitcast.16) | data formatting | bytes 16777216
  17.7 6.2 %slice = bf16[12,32,8192]{2,1,0:T(8,128)(2,1)} slice(bf16[16,32,8192]{2,1,0:T(8,128)(2,1)} %bitcast.15), slice={[0:12], [0:32], [0:8192]} | slice | bytes 12582912 | tf_op jit(solution)/shard_map/reshape | solution.py:13
  23.9 6.3 %copy.8 = bf16[12,32,8192]{2,0,1:T(8,128)(2,1)S(1)} copy(bf16[12,32,8192]{2,1,0:T(8,128)(2,1)} %slice) | data formatting | bytes 12582912 | tf_op jit(solution)/shard_map/reshape | solution.py:13
  30.3 102.9 %all_to_all.15 = bf16[12,32,8192]{2,0,1:T(8,128)(2,1)} all-to-all(bf16[12,32,8192]{2,0,1:T(8,128)(2,1)S(1)} %copy.8), channel_id=1, replica_groups=mesh['grp'=4,'mem'=32] {'mem'}, dimensions={1} | all-to-all | bytes 12582912 | tf_op jit(solution)/shard_map/all_to_all | solution.py:14
  133.2 0.0 copy-start
  133.2 0.0 copy-start.1
  133.2 8.8 %reshape.10 = bf16[384,8192]{1,0:T(8,128)(2,1)} reshape(bf16[32,12,1,8192]{3,1,0,2:T(8,128)(2,1)} %bitcast.14) | data formatting | bytes 12582912 | tf_op jit(solution)/shard_map/reshape | solution.py:16
  141.9 0.0 copy-done
  142.0 0.0 copy-done.1
  142.0 0.0 copy-start.2
  142.0 18.9 %fusion.4 = f32[384,1024]{0,1:T(8,128)} fusion(bf16[384,8192]{1,0:T(8,128)(2,1)} %reshape.10, bf16[8192,1024]{1,0:T(8,128)(2,1)} %param.5, s32[1024]{0:T(1024)S(1)} %copy-done.1, s32[8192]{0:T(1024)S(1)} %copy-done), kind=kOutput, calls=%fused_computation.5 | convolution fusion | flops 6459228160 | bytes 24678400 | tf_op jit(solution)/shard_map/dot_general | solution.py:15
  160.8 0.0 all-reduce.3.cloned.1.call-update
  160.9 0.0 reduce-scatter.3.cloned.1.call-start
  160.9 0.0 copy-done.2
  160.9 0.6 dynamic-slice
  162.2 302.6 %all-reduce.3.cloned.1.call-done = f32[384,1024]{0,1:T(8,128)} async-done(((f32[384,1024]{0,1:T(8,128)}), f32[384,1024]{0,1:T(8,128)}) %all-reduce.3.cloned.1.call-update) | async-done | bytes 1572880
  464.7 2.2 constant_dynamic-slice_fusion
  466.9 0.0 reduce-scatter.3.cloned.1.call-update
  467.0 37.4 %reduce-scatter.3.cloned.1.call-done = f32[12,256]{0,1:T(8,128)} async-done(((f32[12,1024]{0,1:T(8,128)}), f32[12,256]{0,1:T(8,128)}) %reduce-scatter.3.cloned.1.call-update) | async-done | bytes 12304 | tf_op jit(solution)/shard_map/reduce_scatter | solution.py:19
  504.4 1.6 copy.9
Async XLA Ops:
  6.5 458.2 %all-reduce.3.cloned.1.call-start = ((), (), s32[]{:S(2)}) async-start(), calls=%async_computation.3 | async-start | bytes 3145728
  133.2 8.8 %copy-start = (s32[8192]{0:T(1024)S(1)}, s32[8192]{0:T(1024)}, u32[]{:S(2)}) copy-start(s32[8192]{0:T(1024)} %param.6) | copy-start | bytes 98308
  133.2 8.8 %copy-start.1 = (s32[1024]{0:T(1024)S(1)}, s32[1024]{0:T(1024)}, u32[]{:S(2)}) copy-start(s32[1024]{0:T(1024)} %param.7) | copy-start | bytes 12292
  142.0 19.0 %copy-start.2 = (u32[128]{0:T(128)S(1)}, u32[128]{0:T(128)}, u32[]{:S(2)}) copy-start(u32[128]{0:T(128)} %constant.5) | copy-start | bytes 1540
  160.9 343.5 %reduce-scatter.3.cloned.1.call-start = ((), (), s32[]{:S(2)}) async-start(), calls=%async_computation.2 | async-start | bytes 655360 | tf_op jit(solution)/shard_map/reduce_scatter | solution.py:19
Sparse Core Ops, SparseCore 0:
  161.0 303.6 all-reduce.2
  467.5 36.8 reduce-scatter.2
where the time goes:
time: 514 us; the launch traced here: 513 us
  waiting for transfers between devices  340 us (66%)
  blocking collectives  103 us (20%)
  local copies, waits for them, and re-layouts  36.9 us (7%)
  matrix products  18.9 us (4%)
  between operations  14.1 us (3%)
    unnamed x3, waiting for transfers between devices  303 us
    all_to_all x1, blocking collectives, local(): lax.all_to_all(shaped, 'mem', split_axis=1, concat_axis=0, tiled=True)  103 us
    reduce_scatter x1, waiting for transfers between devices, local(): result = lax.psum_scatter(row_share, 'grp', scatter_dimension=1, tiled=True)  37.4 us
    dot_general x1, matrix products, local(): jnp.dot(arrived.reshape(-1, pair_cols), blocked, preferred_element_type=j...  18.9 us
    unnamed x9, local copies, waits for them, and re-layouts  14 us
    reshape x2, local copies, waits for them, and re-layouts, local(): shaped = amplitudes.reshape(own_rows, member_count, pair_cols)  12.5 us
  transfers between devices with their start and end apart: 2, of which 2 were waited for; matrix products, arithmetic and copies ran while one was open for 0% of the time, Pallas kernels for 0%

commit v1 on v0

v1 whole, which is shorter than its diff:
```python
import functools

import jax
import jax.numpy as jnp
from jax import lax
from jax.experimental import pallas as pl
from jax.experimental.pallas import tpu as pltpu
from jax.sharding import PartitionSpec as P

MESH = pl.DeviceIdType.MESH
SIDE = 4
GROUPS = 4
SLOTS = 8
HIGH = 8
CHUNKS = 4
AHEAD = 2


def kernel(
    rows, width,
    amp, integ, ef_ref, ab_ref, out_ref,
    got, blocked, acc, sib, chip, zgot, final, total,
    send_sem, recv_sem, self_sem, integ_sem,
    sib_send, sib_recv, z_send, z_recv, fin_send, fin_recv,
):
    low = rows - HIGH
    me, grp = lax.axis_index("mem"), lax.axis_index("grp")
    x, y, z = me // 8, lax.rem(me // 2, 4), lax.rem(me, 2)
    z_hi, core = grp // 2, lax.rem(grp, 2)
    piece = width // CHUNKS
    cols = integ.shape[1] // 4

    def own_copy(half):
        count = HIGH if half == 0 else low
        return pltpu.make_async_copy(
            amp.at[pl.ds(half * HIGH, count), pl.ds(pl.multiple_of(me * width, 128), width)],
            got.at[0, z, half, pl.ds(0, count)],
            self_sem.at[half],
        )

    def integ_copy(c):
        span = pl.ds(c * piece, piece)
        return pltpu.make_async_copy(integ.at[span], blocked.at[span], integ_sem.at[c])

    own_copy(0).start()
    own_copy(1).start()
    for c in range(CHUNKS):
        integ_copy(c).start()

    barrier = pltpu.get_barrier_semaphore()

    @pl.loop(1, 32)
    def _(step):
        pl.semaphore_signal(barrier, inc=1, device_id={"mem": lax.rem(me + step, 32)}, device_id_type=MESH)

    sibling = {"grp": z_hi * 2 + 1 - core}
    partner = {"grp": (1 - z_hi) * 2 + core, "mem": me + 1 - 2 * z}
    pl.semaphore_signal(barrier, inc=1, device_id=sibling, device_id_type=MESH)
    pl.semaphore_signal(barrier, inc=1, device_id=partner, device_id_type=MESH)
    pl.semaphore_wait(barrier, 33)

    def send(k, c):
        @pl.loop(0, SLOTS)
        def _(j):
            first = j // 2
            e = (1 - core) * first + core * lax.rem(SIDE - first, SIDE)
            target = lax.rem(x + e, SIDE) * 8 + lax.rem(y + e + k, SIDE) * 2 + lax.rem(j, 2)

            @pl.when(target != me)
            def _():
                span = pl.ds(pl.multiple_of(target * width + c * piece, 128), piece)
                there = pl.ds(c * piece, piece)
                for half, count in ((0, HIGH), (1, low)):
                    pltpu.make_async_remote_copy(
                        src_ref=amp.at[pl.ds(half * HIGH, count), span],
                        dst_ref=got.at[k, e * 2 + z, half, pl.ds(0, count), there],
                        send_sem=send_sem.at[k, half],
                        recv_sem=recv_sem.at[k, c, half],
                        device_id={"mem": target},
                        device_id_type=MESH,
                    ).start()

    for k in range(AHEAD):
        for c in range(CHUNKS):
            send(k, c)

    def settle(ref, sem):
        pltpu.make_async_copy(ref, ref, sem).wait()

    def mask(c):
        integ_copy(c).wait()

        @pl.loop(c * (piece // 128), (c + 1) * (piece // 128))
        def _(b):
            label = ef_ref[pl.ds(b, 1), :].astype(jnp.float32)
            column = jnp.broadcast_to(label, (128, 128)).T
            here = pl.ds(pl.multiple_of(b * 128, 128), 128)
            for n in range(integ.shape[1] // 128):
                row = ab_ref[pl.ds(n, 1), :].astype(jnp.float32)
                allowed = (column == row).astype(jnp.float32).astype(jnp.bfloat16)
                lanes = pl.ds(n * 128, 128)
                blocked[here, lanes] = blocked[here, lanes] * allowed

    def multiply(k, c):
        count = SLOTS - 1 if k == 0 else SLOTS
        there = pl.ds(c * piece, piece)
        settle(got.at[k, pl.ds(0, count), 0, :, there], recv_sem.at[k, c, 0])
        settle(got.at[k, pl.ds(0, count), 1, pl.ds(0, low), there], recv_sem.at[k, c, 1])
        left = got[k, :, :, :, there].astype(jnp.float32).reshape(SLOTS * 16, piece).astype(jnp.bfloat16)

        @pl.loop(0, 4)
        def _(g):
            right = blocked[there, pl.ds(pl.multiple_of(g * cols, 128), cols)]
            product = jnp.dot(left, right, preferred_element_type=jnp.float32)
            if c == 0:
                acc[k, g] = product
            else:
                acc[k, g] += product

    def sib_copy(k, zh):
        return pltpu.make_async_remote_copy(
            src_ref=acc.at[k, zh * 2 + 1 - core], dst_ref=sib.at[k, zh],
            send_sem=sib_send.at[k, zh], recv_sem=sib_recv.at[k, zh],
            device_id=sibling, device_id_type=MESH,
        )

    def z_copy(k):
        return pltpu.make_async_remote_copy(
            src_ref=chip.at[k, 1 - z_hi], dst_ref=zgot.at[k],
            send_sem=z_send.at[k], recv_sem=z_recv.at[k],
            device_id=partner, device_id_type=MESH,
        )

    def reduce_start(k):
        sib_copy(k, 0).start()
        sib_copy(k, 1).start()

    def reduce_mid(k):
        for zh in range(2):
            sib_copy(k, zh).wait()
            chip[k, zh] = acc[k, zh * 2 + core] + sib[k, zh]
        z_copy(k).start()

    def reduce_end(k):
        z_copy(k).wait()
        chip[k, z_hi] = chip[k, z_hi] + zgot[k]

        @pl.loop(0, SLOTS)
        def _(j):
            e = j // 2
            owner = lax.rem(x - e + SIDE, SIDE) * 8 + lax.rem(y - e - k + 2 * SIDE, SIDE) * 2 + lax.rem(j, 2)

            @pl.when(owner != me)
            def _():
                for half, count in ((0, HIGH), (1, low)):
                    pltpu.make_async_remote_copy(
                        src_ref=chip.at[k, z_hi, pl.ds(pl.multiple_of(j * 16 + half * HIGH, 8), count)],
                        dst_ref=final.at[k, e * 2 + z, half, pl.ds(0, count)],
                        send_sem=fin_send.at[k, half],
                        recv_sem=fin_recv.at[k, half],
                        device_id={"mem": owner},
                        device_id_type=MESH,
                    ).start()

            @pl.when(owner == me)
            def _():
                for half in range(2):
                    final[k, e * 2 + z, half] = chip[k, z_hi, pl.ds(pl.multiple_of(j * 16 + half * HIGH, 8), HIGH)]

    def collect(k):
        count = SLOTS - 1 if k == 0 else SLOTS
        settle(final.at[k, pl.ds(0, count), 0], fin_recv.at[k, 0])
        settle(final.at[k, pl.ds(0, count), 1, pl.ds(0, low)], fin_recv.at[k, 1])
        added = final[k, 0]
        for s in range(1, SLOTS):
            added = added + final[k, s]
        if k == 0:
            total[...] = added
        else:
            total[...] += added

    for k in range(GROUPS):
        for c in range(CHUNKS):
            if k == 0:
                mask(c)
                if c == 0:
                    own_copy(0).wait()
                    own_copy(1).wait()
            multiply(k, c)
            if k + AHEAD < GROUPS:
                send(k + AHEAD, c)
            if k > 0 and c == 0:
                reduce_mid(k - 1)
            if k > 0 and c == 2:
                reduce_end(k - 1)
        reduce_start(k)
    last = GROUPS - 1
    reduce_mid(last)
    for k in range(GROUPS):
        count = SLOTS - 1 if k == 0 else SLOTS
        settle(got.at[k, pl.ds(0, count), 0], send_sem.at[k, 0])
        settle(got.at[k, pl.ds(0, count), 1, pl.ds(0, low)], send_sem.at[k, 1])
    for k in range(last):
        collect(k)
    reduce_end(last)
    collect(last)
    for k in range(GROUPS):
        count = SLOTS - 1 if k == 0 else SLOTS
        settle(final.at[k, pl.ds(0, count), 0], fin_send.at[k, 0])
        settle(final.at[k, pl.ds(0, count), 1, pl.ds(0, low)], fin_send.at[k, 1])
    out_ref[pl.ds(0, HIGH), :] = total[0]
    out_ref[pl.ds(HIGH, low), :] = total[1, pl.ds(0, low), :]


def local(amplitudes, integrals, irrep_ef, irrep_ab):
    rows, (width, ab) = amplitudes.shape[0], integrals.shape
    cols = ab // 4
    dma, vmem = pltpu.SemaphoreType.DMA, pltpu.VMEM
    return pl.pallas_call(
        functools.partial(kernel, rows, width),
        out_shape=jax.ShapeDtypeStruct((rows, cols), jnp.float32),
        in_specs=[
            pl.BlockSpec(memory_space=pl.ANY),
            pl.BlockSpec(memory_space=pl.ANY),
            pl.BlockSpec(memory_space=vmem),
            pl.BlockSpec(memory_space=vmem),
        ],
        out_specs=pl.BlockSpec(memory_space=vmem),
        scratch_shapes=[
            vmem((GROUPS, SLOTS, 2, HIGH, width), jnp.bfloat16),
            vmem((width, ab), jnp.bfloat16),
            vmem((GROUPS, 4, SLOTS * 16, cols), jnp.float32),
            vmem((GROUPS, 2, SLOTS * 16, cols), jnp.float32),
            vmem((GROUPS, 2, SLOTS * 16, cols), jnp.float32),
            vmem((GROUPS, SLOTS * 16, cols), jnp.float32),
            vmem((GROUPS, SLOTS, 2, HIGH, cols), jnp.float32),
            vmem((2, HIGH, cols), jnp.float32),
            dma((GROUPS, 2)), dma((GROUPS, CHUNKS, 2)), dma((2,)), dma((CHUNKS,)),
            dma((GROUPS, 2)), dma((GROUPS, 2)), dma((GROUPS,)), dma((GROUPS,)),
            dma((GROUPS, 2)), dma((GROUPS, 2)),
        ],
        compiler_params=pltpu.CompilerParams(
            collective_id=0, has_side_effects=True, vmem_limit_bytes=56 * 2**20
        ),
    )(amplitudes, integrals, irrep_ef.reshape(-1, 128), irrep_ab.reshape(-1, 128))


def solution(mesh):
    placed = (P("mem", "grp"), P(("grp", "mem"), None), P(("grp", "mem")), P())
    return jax.shard_map(
        local, mesh=mesh, in_specs=placed, out_specs=P("mem", "grp"), check_vma=False
    )
```

time: 514 us -> 109 us (0.21)
  the two profiles are of different devices: /device:TPU:2 before, /device:TPU:68 now
where the time goes in v1:
time: 109 us
  Pallas kernels  108 us (99%)
  local copies, waits for them, and re-layouts  1.32 us (1%)
    pallas_call x1, Pallas kernels, local(): pl.pallas_call(functools.partial(kernel, rows, width), out_shape=jax.Shap...  108 us

profile of v1, /device:TPU:68, one launch (start us, length us, event | category | flops | bytes accessed | tf_op | source)
XLA Modules:
  0.0 108.9 jit_solution(10070534716383341069)
XLA Ops:
  0.0 107.5 %shard_map.46 = f32[12,256]{1,0:T(8,128)} custom-call(bf16[12,262144]{1,0:T(8,128)(2,1)} %amp.1, bf16[8192,1024]{1,0:T(8,128)(2,1)} %integ.1, s32[64,128]{1,0:T(8,128)} %bitcast.2, s32[8,128]{1,0:T(8,128)} %bitcast.3), custom_call_target="tpu_custom_call" | custom-call | tf_op jit(solution)/shard_map/pallas_call | solution.py:219
  107.5 1.3 %copy.6 = f32[12,256]{1,0:T(8,128)} copy(f32[12,256]{1,0:T(8,128)} %shard_map.46) | data formatting | bytes 24576

commit v2 on v0

v2 whole, which is shorter than its diff:
```python
import functools

import jax
import jax.numpy as jnp
from jax import lax
from jax.experimental import pallas as pl
from jax.experimental.pallas import tpu as pltpu
from jax.sharding import PartitionSpec as P

MESH = pl.DeviceIdType.MESH
SIDE = 4
HIGH = 8
GROUPS = [[(0, 0), (2, 2), (1, 1), (3, 3)], [(0, 1), (0, 3), (2, 1), (2, 3)], [(1, 0), (3, 0), (1, 2), (3, 2)], [(0, 2), (2, 0)], [(1, 3), (3, 1)]]
PIECES = [4, 4, 4, 4, 4]
AHEAD = 6
LAG = 5
FIRST = [sum(len(g) for g in GROUPS[:k]) for k in range(len(GROUPS) + 1)]
ENTRIES = FIRST[-1]
LAST = len(GROUPS) - 1


def mirror(group, n):
    dx, dy = group[n]
    for want in ((-dx % SIDE, -dy % SIDE), (-dx % SIDE, None)):
        for m, (a, b) in enumerate(group):
            if a == want[0] and want[1] in (None, b):
                return m
    return n


def kernel(
    rows, width,
    amp, integ, ef_ref, ab_ref, out_ref,
    got, blocked, acc, sib, chip, zgot, final, direct, total,
    send_sem, recv_sem, self_sem, integ_sem, all_sem,
    sib_send, sib_recv, z_send, z_recv, fin_send, fin_recv, dir_send, dir_recv,
):
    low = rows - HIGH
    me, grp = lax.axis_index("mem"), lax.axis_index("grp")
    x, y, z = me // 8, lax.rem(me // 2, SIDE), lax.rem(me, 2)
    z_hi, core = grp // 2, lax.rem(grp, 2)
    cols = integ.shape[1] // 4
    halves = ((0, HIGH), (1, low))
    mask_pieces = 4

    def own_copy(half, count):
        return pltpu.make_async_copy(
            amp.at[pl.ds(half * HIGH, count), pl.ds(pl.multiple_of(me * width, 128), width)],
            got.at[z, half, pl.ds(0, count)],
            self_sem.at[half],
        )

    def integ_copy(c):
        span = pl.ds(c * (width // mask_pieces), width // mask_pieces)
        return pltpu.make_async_copy(integ.at[span], blocked.at[span], integ_sem.at[c])

    barrier = pltpu.get_barrier_semaphore()

    @pl.loop(1, 32)
    def _(step):
        pl.semaphore_signal(barrier, inc=1, device_id={"mem": lax.rem(me + step, 32)}, device_id_type=MESH)

    for step in range(1, 4):
        pl.semaphore_signal(barrier, inc=1, device_id={"grp": lax.rem(grp + step, 4)}, device_id_type=MESH)
    for half, count in halves:
        own_copy(half, count).start()
    for c in range(mask_pieces):
        integ_copy(c).start()
    acc[...] = jnp.zeros_like(acc)
    pl.semaphore_wait(barrier, 34)

    sibling = {"grp": z_hi * 2 + 1 - core}
    partner = {"grp": (1 - z_hi) * 2 + core, "mem": me + 1 - 2 * z}

    def pick(group, n):
        m = mirror(group, n)
        (a, b), (c, d) = group[n], group[m]
        if m == n:
            return n, a, b
        return n + core * (m - n), a + core * (c - a), b + core * (d - b)

    def send(k, c):
        piece = width // PIECES[k]
        there = pl.ds(c * piece, piece)
        group = GROUPS[k]
        for n, dz in [(n, (n + r) % 2) for r in range(2) for n in range(len(group))]:
            if group[n] == (0, 0) and dz == 0:
                continue
            place, dx, dy = pick(group, n)
            target = lax.rem(x + dx, SIDE) * 8 + lax.rem(y + dy, SIDE) * 2 + lax.rem(z + dz, 2)
            span = pl.ds(pl.multiple_of(target * width + c * piece, 128), piece)
            for half, count in halves:
                pltpu.make_async_remote_copy(
                    src_ref=amp.at[pl.ds(half * HIGH, count), span],
                    dst_ref=got.at[(FIRST[k] + place) * 2 + z, half, pl.ds(0, count), there],
                    send_sem=send_sem.at[k, half],
                    recv_sem=recv_sem.at[k, c, half],
                    device_id={"mem": target},
                    device_id_type=MESH,
                ).start()

    def settle(ref, sem):
        pltpu.make_async_copy(ref, ref, sem).wait()

    def settle_rows(ref, k, sem, *there):
        slots = pl.ds(FIRST[k] * 2, len(GROUPS[k]) * 2 - ((0, 0) in GROUPS[k]))
        for half, count in halves:
            settle(ref.at[(slots, half, pl.ds(0, count), *there)], sem(half))

    def mask(c):
        integ_copy(c).wait()
        blocks = width // mask_pieces // 128

        @pl.loop(c * blocks, (c + 1) * blocks)
        def _(b):
            label = ef_ref[pl.ds(b, 1), :].astype(jnp.float32)
            column = jnp.broadcast_to(label, (128, 128)).T
            here = pl.ds(pl.multiple_of(b * 128, 128), 128)
            for n in range(integ.shape[1] // 128):
                row = ab_ref[pl.ds(n, 1), :].astype(jnp.float32)
                allowed = (column == row).astype(jnp.float32).astype(jnp.bfloat16)
                lanes = pl.ds(n * 128, 128)
                blocked[here, lanes] = blocked[here, lanes] * allowed

    def span_of(k):
        return pl.ds(FIRST[k] * 32, len(GROUPS[k]) * 32)

    def arrive(k, c):
        piece = width // PIECES[k]
        settle_rows(got, k, lambda half: recv_sem.at[k, c, half], pl.ds(c * piece, piece))

    def multiply(k, c):
        piece = width // PIECES[k]
        deep = min(piece, 2048)

        @pl.loop(0, piece // deep)
        def _(part):
            there = pl.ds(pl.multiple_of(c * piece + part * deep, 128), deep)
            left = got[pl.ds(FIRST[k] * 2, len(GROUPS[k]) * 2), :, :, there].astype(jnp.float32)
            left = left.reshape(len(GROUPS[k]) * 32, deep).astype(jnp.bfloat16)
            product = jnp.dot(left, blocked[there, :], preferred_element_type=jnp.float32)
            for g in range(4):
                acc[g, span_of(k)] += product[:, g * cols : (g + 1) * cols]

    def sib_copy(k, zh):
        return pltpu.make_async_remote_copy(
            src_ref=acc.at[zh * 2 + 1 - core, span_of(k)], dst_ref=sib.at[zh, span_of(k)],
            send_sem=sib_send.at[k, zh], recv_sem=sib_recv.at[k, zh],
            device_id=sibling, device_id_type=MESH,
        )

    def z_copy(k):
        return pltpu.make_async_remote_copy(
            src_ref=chip.at[1 - z_hi, span_of(k)], dst_ref=zgot.at[span_of(k)],
            send_sem=z_send.at[k], recv_sem=z_recv.at[k],
            device_id=partner, device_id_type=MESH,
        )

    def reduce_start(k):
        sib_copy(k, 0).start()
        sib_copy(k, 1).start()

    def reduce_mid(k):
        for zh in range(2):
            sib_copy(k, zh).wait()
            chip[zh, span_of(k)] = acc[zh * 2 + core, span_of(k)] + sib[zh, span_of(k)]
        z_copy(k).start()

    def owner_of(k, n, zs):
        dx, dy = GROUPS[k][n]
        return lax.rem(x + SIDE - dx, SIDE) * 8 + lax.rem(y + SIDE - dy, SIDE) * 2 + zs

    def reduce_end(k):
        z_copy(k).wait()
        chip[z_hi, span_of(k)] = chip[z_hi, span_of(k)] + zgot[span_of(k)]
        for n in range(len(GROUPS[k])):
            for zs in range(2):
                owner = owner_of(k, n, zs)
                top = (FIRST[k] + n) * 32 + zs * 16

                def start(owner=owner, top=top, n=n):
                    for half, count in halves:
                        pltpu.make_async_remote_copy(
                            src_ref=chip.at[z_hi, pl.ds(top + half * HIGH, count)],
                            dst_ref=final.at[(FIRST[k] + n) * 2 + z, half, pl.ds(0, count)],
                            send_sem=fin_send.at[k, half],
                            recv_sem=fin_recv.at[k, half],
                            device_id={"mem": owner},
                            device_id_type=MESH,
                        ).start()

                def keep(top=top, n=n):
                    for half, count in halves:
                        final[(FIRST[k] + n) * 2 + z, half] = chip[z_hi, pl.ds(top + half * HIGH, HIGH)]

                if GROUPS[k][n] == (0, 0):
                    pl.when(owner != me)(start)
                    pl.when(owner == me)(keep)
                else:
                    start()

    def collect(k):
        settle_rows(final, k, lambda half: fin_recv.at[k, half])
        added = final[FIRST[k] * 2]
        for slot in range(FIRST[k] * 2 + 1, FIRST[k + 1] * 2):
            added = added + final[slot]
        total[...] = total[...] + added if k else added

    def direct_start(k):
        @pl.loop(0, 4)
        def _(g):
            for n in range(len(GROUPS[k])):
                for zs in range(2):
                    top = (FIRST[k] + n) * 32 + zs * 16
                    for half, count in halves:
                        pltpu.make_async_remote_copy(
                            src_ref=acc.at[g, pl.ds(top + half * HIGH, count)],
                            dst_ref=direct.at[n, z, grp, half, pl.ds(0, count)],
                            send_sem=dir_send.at[half],
                            recv_sem=dir_recv.at[half],
                            device_id={"grp": g, "mem": owner_of(k, n, zs)},
                            device_id_type=MESH,
                        ).start()

    def settle_direct(sem):
        for half, count in halves:
            settle(direct.at[:, :, :, half, pl.ds(0, count)], sem.at[half])

    steps = [(k, c) for k in range(LAST + 1) for c in range(PIECES[k])]
    for k, c in steps[:AHEAD]:
        send(k, c)
    for step in range(1, 4):
        pl.semaphore_signal(all_sem, inc=1, device_id={"grp": lax.rem(grp + step, 4)}, device_id_type=MESH)
    for c in range(mask_pieces):
        mask(c)
    for half, count in halves:
        own_copy(half, count).wait()
    pl.semaphore_wait(all_sem, 3)
    ends = {k: sum(PIECES[: k + 1]) - 1 for k in range(LAST)}
    for i, (k, c) in enumerate(steps):
        arrive(k, c)
        if i + AHEAD < len(steps):
            send(*steps[i + AHEAD])
        for old, end in ends.items():
            if i == end + LAG:
                reduce_mid(old)
            if i == end + 2 * LAG:
                reduce_end(old)
        multiply(k, c)
        if k < LAST and i == ends[k]:
            reduce_start(k)
    direct_start(LAST)
    for old, end in ends.items():
        if end + LAG >= len(steps):
            reduce_mid(old)
    for old, end in ends.items():
        if end + 2 * LAG >= len(steps):
            reduce_end(old)
    for k in range(LAST + 1):
        settle_rows(got, k, lambda half: send_sem.at[k, half])
    for k in range(LAST):
        collect(k)
    for k in range(LAST):
        settle_rows(final, k, lambda half: fin_send.at[k, half])
    settle_direct(dir_recv)
    for n in range(len(GROUPS[LAST])):
        for zs in range(2):
            for g in range(4):
                total[...] += direct[n, zs, g]
    out_ref[pl.ds(0, HIGH), :] = total[0]
    out_ref[pl.ds(HIGH, low), :] = total[1, pl.ds(0, low), :]
    settle_direct(dir_send)


def local(amplitudes, integrals, irrep_ef, irrep_ab):
    rows, (width, ab) = amplitudes.shape[0], integrals.shape
    cols, deep, n = ab // 4, ENTRIES * 32, LAST + 1
    dma, vmem = pltpu.SemaphoreType.DMA, pltpu.VMEM
    return pl.pallas_call(
        functools.partial(kernel, rows, width),
        out_shape=jax.ShapeDtypeStruct((rows, cols), jnp.float32),
        in_specs=[
            pl.BlockSpec(memory_space=pl.ANY),
            pl.BlockSpec(memory_space=pl.ANY),
            pl.BlockSpec(memory_space=vmem),
            pl.BlockSpec(memory_space=vmem),
        ],
        out_specs=pl.BlockSpec(memory_space=vmem),
        scratch_shapes=[
            vmem((ENTRIES * 2, 2, HIGH, width), jnp.bfloat16),
            vmem((width, ab), jnp.bfloat16),
            vmem((4, deep, cols), jnp.float32),
            vmem((2, deep, cols), jnp.float32),
            vmem((2, deep, cols), jnp.float32),
            vmem((deep, cols), jnp.float32),
            vmem((ENTRIES * 2, 2, HIGH, cols), jnp.float32),
            vmem((len(GROUPS[LAST]), 2, 4, 2, HIGH, cols), jnp.float32),
            vmem((2, HIGH, cols), jnp.float32),
            dma((n, 2)), dma((n, max(PIECES), 2)), dma((2,)), dma((4,)), pltpu.SemaphoreType.REGULAR,
            dma((n, 2)), dma((n, 2)), dma((n,)), dma((n,)),
            dma((n, 2)), dma((n, 2)), dma((2,)), dma((2,)),
        ],
        compiler_params=pltpu.CompilerParams(
            collective_id=0, has_side_effects=True, vmem_limit_bytes=56 * 2**20
        ),
    )(amplitudes, integrals, irrep_ef.reshape(-1, 128), irrep_ab.reshape(-1, 128))


def solution(mesh):
    placed = (P("mem", "grp"), P(("grp", "mem"), None), P(("grp", "mem")), P())
    return jax.shard_map(
        local, mesh=mesh, in_specs=placed, out_specs=P("mem", "grp"), check_vma=False
    )
```

time: 514 us -> 99.2 us (0.19)
  waiting for transfers between devices: 340 us -> 0 us
  blocking collectives: 103 us -> 0 us
  Pallas kernels: 0 us -> 96.2 us
  local copies, waits for them, and re-layouts: 36.9 us -> 1.32 us
  matrix products: 18.9 us -> 0 us
  between operations: 14.1 us -> 0.01 us
    unnamed x3 -> x0, waiting for transfers between devices: 303 us -> none
    all_to_all x1 -> x0, blocking collectives: 103 us -> none  [local(): lax.all_to_all(shaped, 'mem', split_axis=1, concat_axis=0, tiled=True)]
    pallas_call x0 -> x1, Pallas kernels: none -> 96.2 us  [local(): pl.pallas_call(functools.partial(kernel, rows, width), out_shape=jax.Shap...]
    reduce_scatter x1 -> x0, waiting for transfers between devices: 37.4 us -> none  [local(): result = lax.psum_scatter(row_share, 'grp', scatter_dimension=1, tiled=True)]
    reshape x3 -> x0, local copies, waits for them, and re-layouts: 21.3 us -> none  [the longest x2 12.5 us: local(): shaped = amplitudes.reshape(own_rows, member_count, pair_cols)]
    dot_general x1 -> x0, matrix products: 18.9 us -> none  [local(): jnp.dot(arrived.reshape(-1, pair_cols), blocked, preferred_element_type=j...]
    unnamed x9 -> x1, local copies, waits for them, and re-layouts: 14 us -> 1.32 us
  transfers between devices with their start and end apart: 2 -> 0, of which waited for: 2 -> 0; matrix products, arithmetic and copies ran while one was open for 0% -> 0% of each run, Pallas kernels for 0% -> 0%
where the time goes in v2:
time: 99.2 us; the launch traced here: 97.5 us
  Pallas kernels  96.2 us (97%)
  local copies, waits for them, and re-layouts  1.32 us (1%)
    pallas_call x1, Pallas kernels, local(): pl.pallas_call(functools.partial(kernel, rows, width), out_shape=jax.Shap...  96.2 us

profile of v2, /device:TPU:2, one launch (start us, length us, event | category | flops | bytes accessed | tf_op | source)
XLA Modules:
  0.0 97.5 jit_solution(165776287263622855)
XLA Ops:
  0.0 96.2 %shard_map.46 = f32[12,256]{1,0:T(8,128)} custom-call(bf16[12,262144]{1,0:T(8,128)(2,1)} %amp.1, bf16[8192,1024]{1,0:T(8,128)(2,1)} %integ.1, s32[64,128]{1,0:T(8,128)} %bitcast.2, s32[8,128]{1,0:T(8,128)} %bitcast.3), custom_call_target="tpu_custom_call" | custom-call | tf_op jit(solution)/shard_map/pallas_call | solution.py:279
  96.2 1.3 %copy.6 = f32[12,256]{1,0:T(8,128)} copy(f32[12,256]{1,0:T(8,128)} %shard_map.46) | data formatting | bytes 24576

commit v3 on v2

--- a/solution.py
+++ b/solution.py
@@ -13,10 +13,11 @@
 GROUPS = [[(0, 0), (2, 2), (1, 1), (3, 3)], [(0, 1), (0, 3), (2, 1), (2, 3)], [(1, 0), (3, 0), (1, 2), (3, 2)], [(0, 2), (2, 0)], [(1, 3), (3, 1)]]
 PIECES = [4, 4, 4, 4, 4]
 AHEAD = 6
-LAG = 5
+LAG = 7
 FIRST = [sum(len(g) for g in GROUPS[:k]) for k in range(len(GROUPS) + 1)]
 ENTRIES = FIRST[-1]
 LAST = len(GROUPS) - 1
+DEEP = 24
 
 
 def mirror(group, n):
@@ -31,7 +32,7 @@
 def kernel(
     rows, width,
     amp, integ, ef_ref, ab_ref, out_ref,
-    got, blocked, acc, sib, chip, zgot, final, direct, total,
+    got, got_low, blocked, acc, sib, chip, zgot, final, direct, total,
     send_sem, recv_sem, self_sem, integ_sem, all_sem,
     sib_send, sib_recv, z_send, z_recv, fin_send, fin_recv, dir_send, dir_recv,
 ):
@@ -46,7 +47,7 @@
     def own_copy(half, count):
         return pltpu.make_async_copy(
             amp.at[pl.ds(half * HIGH, count), pl.ds(pl.multiple_of(me * width, 128), width)],
-            got.at[z, half, pl.ds(0, count)],
+            got.at[z] if half == 0 else got_low.at[0, pl.ds(z * low, low)],
             self_sem.at[half],
         )
 
@@ -92,7 +93,8 @@
             for half, count in halves:
                 pltpu.make_async_remote_copy(
                     src_ref=amp.at[pl.ds(half * HIGH, count), span],
-                    dst_ref=got.at[(FIRST[k] + place) * 2 + z, half, pl.ds(0, count), there],
+                    dst_ref=got.at[(FIRST[k] + place) * 2 + z, :, there] if half == 0
+                    else got_low.at[FIRST[k] + place, pl.ds(z * low, low), there],
                     send_sem=send_sem.at[k, half],
                     recv_sem=recv_sem.at[k, c, half],
                     device_id={"mem": target},
@@ -102,10 +104,10 @@
     def settle(ref, sem):
         pltpu.make_async_copy(ref, ref, sem).wait()
 
-    def settle_rows(ref, k, sem, *there):
+    def settle_rows(ref, k, sem):
         slots = pl.ds(FIRST[k] * 2, len(GROUPS[k]) * 2 - ((0, 0) in GROUPS[k]))
         for half, count in halves:
-            settle(ref.at[(slots, half, pl.ds(0, count), *there)], sem(half))
+            settle(ref.at[slots, half, pl.ds(0, count)], sem(half))
 
     def mask(c):
         integ_copy(c).wait()
@@ -123,11 +125,16 @@
                 blocked[here, lanes] = blocked[here, lanes] * allowed
 
     def span_of(k):
-        return pl.ds(FIRST[k] * 32, len(GROUPS[k]) * 32)
+        return pl.ds(FIRST[k] * DEEP, len(GROUPS[k]) * DEEP)
+
+    def settle_got(k, sem, there):
+        slots = pl.ds(FIRST[k] * 2, len(GROUPS[k]) * 2 - ((0, 0) in GROUPS[k]))
+        settle(got.at[slots, :, there], sem(0))
+        settle(got.at[slots, pl.ds(0, low), there], sem(1))
 
     def arrive(k, c):
         piece = width // PIECES[k]
-        settle_rows(got, k, lambda half: recv_sem.at[k, c, half], pl.ds(c * piece, piece))
+        settle_got(k, lambda half: recv_sem.at[k, c, half], pl.ds(c * piece, piece))
 
     def multiply(k, c):
         piece = width // PIECES[k]
@@ -136,8 +143,10 @@
         @pl.loop(0, piece // deep)
         def _(part):
             there = pl.ds(pl.multiple_of(c * piece + part * deep, 128), deep)
-            left = got[pl.ds(FIRST[k] * 2, len(GROUPS[k]) * 2), :, :, there].astype(jnp.float32)
-            left = left.reshape(len(GROUPS[k]) * 32, deep).astype(jnp.bfloat16)
+            left = jnp.concatenate([
+                got[pl.ds(FIRST[k] * 2, len(GROUPS[k]) * 2), :, there].astype(jnp.float32).reshape(-1, deep),
+                got_low[pl.ds(FIRST[k], len(GROUPS[k])), :, there].astype(jnp.float32).reshape(-1, deep),
+            ]).astype(jnp.bfloat16)
             product = jnp.dot(left, blocked[there, :], preferred_element_type=jnp.float32)
             for g in range(4):
                 acc[g, span_of(k)] += product[:, g * cols : (g + 1) * cols]
@@ -166,6 +175,11 @@
             chip[zh, span_of(k)] = acc[zh * 2 + core, span_of(k)] + sib[zh, span_of(k)]
         z_copy(k).start()
 
+    def top_of(k, n, zs, half):
+        if half == 0:
+            return FIRST[k] * DEEP + (n * 2 + zs) * HIGH
+        return FIRST[k] * DEEP + len(GROUPS[k]) * 2 * HIGH + n * HIGH + zs * low
+
     def owner_of(k, n, zs):
         dx, dy = GROUPS[k][n]
         return lax.rem(x + SIDE - dx, SIDE) * 8 + lax.rem(y + SIDE - dy, SIDE) * 2 + zs
@@ -176,12 +190,11 @@
         for n in range(len(GROUPS[k])):
             for zs in range(2):
                 owner = owner_of(k, n, zs)
-                top = (FIRST[k] + n) * 32 + zs * 16
-
-                def start(owner=owner, top=top, n=n):
+
+                def start(owner=owner, n=n, zs=zs):
                     for half, count in halves:
                         pltpu.make_async_remote_copy(
-                            src_ref=chip.at[z_hi, pl.ds(top + half * HIGH, count)],
+                            src_ref=chip.at[z_hi, pl.ds(top_of(k, n, zs, half), count)],
                             dst_ref=final.at[(FIRST[k] + n) * 2 + z, half, pl.ds(0, count)],
                             send_sem=fin_send.at[k, half],
                             recv_sem=fin_recv.at[k, half],
@@ -189,9 +202,10 @@
                             device_id_type=MESH,
                         ).start()
 
-                def keep(top=top, n=n):
+                def keep(n=n, zs=zs):
                     for half, count in halves:
-                        final[(FIRST[k] + n) * 2 + z, half] = chip[z_hi, pl.ds(top + half * HIGH, HIGH)]
+                        mine = chip[z_hi, pl.ds(top_of(k, n, zs, half), count)]
+                        final[(FIRST[k] + n) * 2 + z, half, pl.ds(0, count)] = mine
 
                 if GROUPS[k][n] == (0, 0):
                     pl.when(owner != me)(start)
@@ -211,10 +225,9 @@
         def _(g):
             for n in range(len(GROUPS[k])):
                 for zs in range(2):
-                    top = (FIRST[k] + n) * 32 + zs * 16
                     for half, count in halves:
                         pltpu.make_async_remote_copy(
-                            src_ref=acc.at[g, pl.ds(top + half * HIGH, count)],
+                            src_ref=acc.at[g, pl.ds(top_of(k, n, zs, half), count)],
                             dst_ref=direct.at[n, z, grp, half, pl.ds(0, count)],
                             send_sem=dir_send.at[half],
                             recv_sem=dir_recv.at[half],
@@ -257,7 +270,7 @@
         if end + 2 * LAG >= len(steps):
             reduce_end(old)
     for k in range(LAST + 1):
-        settle_rows(got, k, lambda half: send_sem.at[k, half])
+        settle_got(k, lambda half: send_sem.at[k, half], pl.ds(0, width))
     for k in range(LAST):
         collect(k)
     for k in range(LAST):
@@ -274,7 +287,7 @@
 
 def local(amplitudes, integrals, irrep_ef, irrep_ab):
     rows, (width, ab) = amplitudes.shape[0], integrals.shape
-    cols, deep, n = ab // 4, ENTRIES * 32, LAST + 1
+    cols, deep, n = ab // 4, ENTRIES * DEEP, LAST + 1
     dma, vmem = pltpu.SemaphoreType.DMA, pltpu.VMEM
     return pl.pallas_call(
         functools.partial(kernel, rows, width),
@@ -287,7 +300,8 @@
         ],
         out_specs=pl.BlockSpec(memory_space=vmem),
         scratch_shapes=[
-            vmem((ENTRIES * 2, 2, HIGH, width), jnp.bfloat16),
+            vmem((ENTRIES * 2, HIGH, width), jnp.bfloat16),
+            vmem((ENTRIES, HIGH, width), jnp.bfloat16),
             vmem((width, ab), jnp.bfloat16),
             vmem((4, deep, cols), jnp.float32),
             vmem((2, deep, cols), jnp.float32),

time: 99.2 us -> 96.3 us (0.971); the launches traced: 97.5 us -> 96.1 us
  Pallas kernels: 96.2 us -> 94.8 us
    pallas_call x1, Pallas kernels: 96.2 us -> 94.8 us  [local(): pl.pallas_call(functools.partial(kernel, rows, width), out_shape=jax.Shap...]
where the time goes in v3:
time: 96.3 us; the launch traced here: 96.1 us
  Pallas kernels  94.8 us (98%)
  local copies, waits for them, and re-layouts  1.32 us (1%)
    pallas_call x1, Pallas kernels, local(): pl.pallas_call(functools.partial(kernel, rows, width), out_shape=jax.Shap...  94.8 us

profile of v3, /device:TPU:2, one launch (start us, length us, event | category | flops | bytes accessed | tf_op | source)
XLA Modules:
  0.0 96.1 jit_solution(8101422724964987882)
XLA Ops:
  0.0 94.8 %shard_map.46 = f32[12,256]{1,0:T(8,128)} custom-call(bf16[12,262144]{1,0:T(8,128)(2,1)} %amp.1, bf16[8192,1024]{1,0:T(8,128)(2,1)} %integ.1, s32[64,128]{1,0:T(8,128)} %bitcast.2, s32[8,128]{1,0:T(8,128)} %bitcast.3), custom_call_target="tpu_custom_call" | custom-call | tf_op jit(solution)/shard_map/pallas_call | solution.py:292
  94.8 1.3 %copy.6 = f32[12,256]{1,0:T(8,128)} copy(f32[12,256]{1,0:T(8,128)} %shard_map.46) | data formatting | bytes 24576

commit v4 on v3

--- a/solution.py
+++ b/solution.py
@@ -13,7 +13,7 @@
 GROUPS = [[(0, 0), (2, 2), (1, 1), (3, 3)], [(0, 1), (0, 3), (2, 1), (2, 3)], [(1, 0), (3, 0), (1, 2), (3, 2)], [(0, 2), (2, 0)], [(1, 3), (3, 1)]]
 PIECES = [4, 4, 4, 4, 4]
 AHEAD = 6
-LAG = 7
+LAG = 8
 FIRST = [sum(len(g) for g in GROUPS[:k]) for k in range(len(GROUPS) + 1)]
 ENTRIES = FIRST[-1]
 LAST = len(GROUPS) - 1
@@ -84,7 +84,7 @@
         piece = width // PIECES[k]
         there = pl.ds(c * piece, piece)
         group = GROUPS[k]
-        for n, dz in [(n, (n + r) % 2) for r in range(2) for n in range(len(group))]:
+        for n, dz in [(n, (n + r + c) % 2) for r in range(2) for n in range(len(group))]:
             if group[n] == (0, 0) and dz == 0:
                 continue
             place, dx, dy = pick(group, n)

time: 96.3 us -> 96.3 us (level)
  no operation moved by 1% of the time
where the time goes in v4:
time: 96.3 us; the launch traced here: 95.6 us
  Pallas kernels  94.3 us (98%)
  local copies, waits for them, and re-layouts  1.32 us (1%)
    pallas_call x1, Pallas kernels, local(): pl.pallas_call(functools.partial(kernel, rows, width), out_shape=jax.Shap...  94.3 us

profile of v4, /device:TPU:2, one launch (start us, length us, event | category | flops | bytes accessed | tf_op | source)
XLA Modules:
  0.0 95.6 jit_solution(4957503851749906187)
XLA Ops:
  0.0 94.3 %shard_map.46 = f32[12,256]{1,0:T(8,128)} custom-call(bf16[12,262144]{1,0:T(8,128)(2,1)} %amp.1, bf16[8192,1024]{1,0:T(8,128)(2,1)} %integ.1, s32[64,128]{1,0:T(8,128)} %bitcast.2, s32[8,128]{1,0:T(8,128)} %bitcast.3), custom_call_target="tpu_custom_call" | custom-call | tf_op jit(solution)/shard_map/pallas_call | solution.py:292
  94.3 1.3 %copy.6 = f32[12,256]{1,0:T(8,128)} copy(f32[12,256]{1,0:T(8,128)} %shard_map.46) | data formatting | bytes 24576
